TPU v7x, 32 devices: a whole 2x2x4 slice. The times are simulated.
32 devices in a mesh: dp: 8 (over z, y), upd: 4 (over x, core).
Axes of the slice: x: 2, y: 2, z: 4, core: 2. Of those that a mesh axis runs over, the one named last changes fastest.
Arguments:
- inputs: bfloat16 [256, 128, 768], P(('dp', 'upd')), may hold values from -6 to 6
- memory: bfloat16 [256, 256, 768], P(('dp', 'upd')), may hold values from -6 to 6
- cotangent: bfloat16 [256, 128, 768], P(('dp', 'upd')), may hold values from -6 to 6
- lengths: int32 [256], P(('dp', 'upd')), may hold values from 1 to 128, as said below
- memory_len: int32 [256], P(('dp', 'upd')), may hold values from 64 to 225, as said below
- square_master: float32 [8, 768, 768], P(None, ('dp', 'upd')), may hold values from -0.21875 to 0.21875
- tall_master: float32 [2, 3072, 768], P(None, ('dp', 'upd'))
- square_momentum: float32 [8, 768, 768], P(None, ('dp', 'upd'))
- tall_momentum: float32 [2, 3072, 768], P(None, ('dp', 'upd'))
- vectors: bfloat16 [17, 768], replicated, may hold values from -1.5 to 1.5
- feed_vectors: bfloat16 [3, 3072], replicated, may hold values from -1.5 to 1.5
- head_scale: bfloat16 [12], replicated, may hold values from 0.25 to 1.75
- relative: bfloat16 [12, 128], replicated, may hold values from -4 to 4
Outputs:
- output: bfloat16 [256, 128, 768], P(('dp', 'upd'))
- input_gradient: bfloat16 [256, 128, 768], P(('dp', 'upd'))
- memory_gradient: bfloat16 [256, 256, 768], P(('dp', 'upd'))
- square_state: float32 [8, 768, 768], P(None, ('dp', 'upd'))
- tall_state: float32 [2, 3072, 768], P(None, ('dp', 'upd'))
- square_weight: float32 [8, 768, 768], P(None, ('dp', 'upd'))
- tall_weight: float32 [2, 3072, 768], P(None, ('dp', 'upd'))
- vector_gradient: float32 [17, 768], P(None, ('dp', 'upd'))
- feed_gradient: float32 [3, 3072], P(None, ('dp', 'upd'))
- scale_gradient: float32 [12], replicated
- bias_gradient: float32 [12, 128], replicated
Inputs may be any that keep to these rules, and one draw needn't show every extreme that they name: `lengths`: positions at or past an item's count are padding; some item has exactly 128. `memory_len`: each item has 64 or 225 real memory rows, the first ones; both occur.
All inputs are finite; a program needn't handle non-finite values.
Results may differ from a plain program's by a relative error of at most 0.02.
Values may be sent and summed in bfloat16 or wider, within the bound.
A program may use at most 384 MiB of HBM per device.

v0:
```python
import jax
import jax.numpy as jnp
from jax import lax
from jax.sharding import PartitionSpec as P

D = 768
FF = 3072
ITERS = 5
NORM_EPSILON = 1e-05
FLOOR_EPSILON = 1e-07
FIRST_TERM = 3.4445
SECOND_TERM = -4.775
THIRD_TERM = 2.0315
MOMENTUM_DECAY = 0.95
LEARN_RATE = 0.8
WEIGHT_DECAY = 0.01
NEGATIVE_LARGE = -1e30


def plain_round(values):
    return lax.optimization_barrier(values.astype(jnp.bfloat16)).astype(jnp.float32)


def same_value(values):
    return values


def value_keep(values):
    return (plain_round(values), None)


def value_pass(kept, slope):
    return (slope,)


def gradient_keep(values):
    return (values, None)


def gradient_round(kept, slope):
    return (plain_round(slope),)


def round_value(values):
    wrapped = jax.custom_vjp(plain_round)
    wrapped.defvjp(value_keep, value_pass)
    return wrapped(values)


def round_gradient(values):
    wrapped = jax.custom_vjp(same_value)
    wrapped.defvjp(gradient_keep, gradient_round)
    return wrapped(values)


def norm_rows(values, gain, shift):
    center = values - jnp.mean(values, axis=-1, keepdims=True)
    spread = jnp.mean(center * center, axis=-1, keepdims=True)
    return center * lax.rsqrt(spread + NORM_EPSILON) * gain + shift


def attend(query, keys, values, allowed, bias):
    scores = jnp.einsum("bqhe,bkhe->bhqk", query, keys) + bias
    scores = jnp.where(allowed, round_gradient(scores), NEGATIVE_LARGE)
    weights = jnp.exp(scores - jnp.max(scores, axis=-1, keepdims=True))
    weights = round_value(weights / jnp.sum(weights, axis=-1, keepdims=True))
    return round_gradient(jnp.einsum("bhqk,bkhe->bqhe", weights, values))


def split_heads(values, head_count):
    return values.reshape(
        values.shape[0], values.shape[1], head_count, values.shape[2] // head_count
    )


def layer_block(
    inputs, memory, memory_len, square, tall, vectors, feed_vectors, head_scale, relative
):
    item_count, query_count, model_width = inputs.shape
    head_count = head_scale.shape[0]
    memory_slots = memory.shape[1]
    normed = round_value(norm_rows(inputs, vectors[0], vectors[1]))
    query = round_gradient(round_value((jnp.matmul(normed, square[0]) + vectors[2]) * 0.125))
    keys = round_gradient(round_value(jnp.matmul(normed, square[1])))
    values = round_gradient(round_value(jnp.matmul(normed, square[2]) + vectors[3]))
    query_index = jnp.arange(query_count)[:, None]
    key_index = jnp.arange(query_count)[None, :]
    distance = jnp.clip(query_index - key_index, 0, query_count - 1)
    position_table = (distance[:, :, None] == jnp.arange(query_count)[None, None, :]).astype(
        jnp.float32
    )
    bias = jnp.einsum("hd,qkd->hqk", relative, position_table)[None]
    mixed = attend(
        split_heads(query, head_count),
        split_heads(keys, head_count),
        split_heads(values, head_count),
        (query_index >= key_index)[None, None],
        bias,
    )
    mixed = (mixed * head_scale[None, None, :, None]).reshape(item_count, query_count, model_width)
    mixed = round_value(norm_rows(mixed, vectors[5], vectors[6]))
    hidden = inputs + round_gradient(jnp.matmul(mixed, square[3]) + vectors[4])
    normed = round_value(norm_rows(hidden, vectors[7], vectors[8]))
    query = round_gradient(round_value((jnp.matmul(normed, square[4]) + vectors[9]) * 0.125))
    keys = round_gradient(round_value(jnp.matmul(memory, square[5])))
    values = round_gradient(round_value(jnp.matmul(memory, square[6]) + vectors[10]))
    allowed = (jnp.arange(memory_slots)[None, :] < memory_len[:, None])[:, None, None, :]
    mixed = attend(
        split_heads(query, head_count),
        split_heads(keys, head_count),
        split_heads(values, head_count),
        allowed,
        0.0,
    )
    mixed = round_value(
        norm_rows(mixed.reshape(item_count, query_count, model_width), vectors[12], vectors[13])
    )
    hidden = hidden + round_gradient(jnp.matmul(mixed, square[7]) + vectors[11])
    normed = round_value(norm_rows(hidden, vectors[14], vectors[15]))
    inner = round_gradient(jnp.matmul(normed, tall[0].T) + feed_vectors[0])
    active = round_value(
        norm_rows(jax.nn.gelu(inner, approximate=False), feed_vectors[1], feed_vectors[2])
    )
    return hidden + round_gradient(jnp.matmul(active, tall[1]) + vectors[16])


def gram_of(block):
    return jnp.einsum("wrd,wre->wde", block, block, precision=lax.Precision.HIGHEST)


def advance(current, gram):
    mixed = jnp.einsum("wrd,wde->wre", current, gram, precision=lax.Precision.HIGHEST)
    second = jnp.einsum("wrd,wde->wre", mixed, gram, precision=lax.Precision.HIGHEST)
    return FIRST_TERM * current + SECOND_TERM * mixed + THIRD_TERM * second


def both_grams(square, tall):
    joined = jnp.concatenate([gram_of(square), gram_of(tall)], axis=0)
    summed = lax.all_gather(
        lax.psum_scatter(joined, ("dp", "upd"), scatter_dimension=1, tiled=True).astype(
            jnp.bfloat16
        ),
        ("dp", "upd"),
        axis=1,
        tiled=True,
    ).astype(jnp.float32)
    return (summed[:8], summed[8:])


def shared_rows(square_state, tall_state):
    square_squares, tall_squares = lax.psum(
        (
            jnp.sum(square_state * square_state, axis=(1, 2)),
            jnp.sum(tall_state * tall_state, axis=(1, 2)),
        ),
        ("dp", "upd"),
    )
    square = square_state * (1.0 / (jnp.sqrt(square_squares) + FLOOR_EPSILON))[:, None, None]
    tall = tall_state * (1.0 / (jnp.sqrt(tall_squares) + FLOOR_EPSILON))[:, None, None]
    first_sweep = 0
    for sweep in range(first_sweep, ITERS):
        square_gram, tall_gram = both_grams(square, tall)
        square = advance(square, square_gram)
        tall = advance(tall, tall_gram)
    return (square, tall)


def local(
    inputs,
    memory,
    cotangent,
    lengths,
    memory_len,
    square_master,
    tall_master,
    square_momentum,
    tall_momentum,
    vectors,
    feed_vectors,
    head_scale,
    relative,
):
    square_copy, tall_copy = (
        lax.all_gather(square_master.astype(jnp.bfloat16), ("dp", "upd"), axis=1, tiled=True),
        lax.all_gather(tall_master.astype(jnp.bfloat16), ("dp", "upd"), axis=1, tiled=True),
    )
    params = (
        square_copy.astype(jnp.float32),
        tall_copy.astype(jnp.float32),
        vectors.astype(jnp.float32),
        feed_vectors.astype(jnp.float32),
        head_scale.astype(jnp.float32),
        relative.astype(jnp.float32),
    )

    def forward(params, inputs_full, memory_full):
        return layer_block(inputs_full, memory_full, memory_len, *params)

    output, pullback = jax.vjp(
        forward, params, inputs.astype(jnp.float32), memory.astype(jnp.float32)
    )
    valid = (jnp.arange(inputs.shape[1])[None, :] < lengths[:, None]).astype(jnp.float32)
    param_slopes, input_slope, memory_slope = pullback(
        cotangent.astype(jnp.float32) * valid[:, :, None]
    )
    square_slope, tall_slope, vector_slope, feed_slope, scale_slope, bias_slope = param_slopes
    total, scale_sum, bias_sum = lax.psum(
        (jnp.sum(lengths).astype(jnp.float32), scale_slope, bias_slope), ("dp", "upd")
    )
    square_sum, tall_sum, vector_sum, feed_sum = (
        lax.psum_scatter(square_slope, ("dp", "upd"), scatter_dimension=1, tiled=True),
        lax.psum_scatter(tall_slope, ("dp", "upd"), scatter_dimension=1, tiled=True),
        lax.psum_scatter(vector_slope, ("dp", "upd"), scatter_dimension=1, tiled=True),
        lax.psum_scatter(feed_slope, ("dp", "upd"), scatter_dimension=1, tiled=True),
    )
    factor = inputs.shape[0] * lax.axis_size("dp") * lax.axis_size("upd") / total
    square_state = MOMENTUM_DECAY * square_momentum + factor * square_sum
    tall_state = MOMENTUM_DECAY * tall_momentum + factor * tall_sum
    square, tall = shared_rows(square_state, tall_state)
    square_weight = square_master * (1.0 - LEARN_RATE * WEIGHT_DECAY) - LEARN_RATE * square
    tall_weight = (
        tall_master * (1.0 - LEARN_RATE * WEIGHT_DECAY)
        - LEARN_RATE * max(1.0, FF / D) ** 0.5 * tall
    )
    return (
        output.astype(jnp.bfloat16),
        input_slope.astype(jnp.bfloat16),
        memory_slope.astype(jnp.bfloat16),
        square_state,
        tall_state,
        square_weight,
        tall_weight,
        factor * vector_sum,
        factor * feed_sum,
        factor * scale_sum,
        factor * bias_sum,
    )


def solution(mesh):
    placed = (
        P(("dp", "upd"), None, None),
        P(("dp", "upd"), None, None),
        P(("dp", "upd"), None, None),
        P(("dp", "upd")),
        P(("dp", "upd")),
        P(None, ("dp", "upd"), None),
        P(None, ("dp", "upd"), None),
        P(None, ("dp", "upd"), None),
        P(None, ("dp", "upd"), None),
        P(),
        P(),
        P(),
        P(),
    )
    return jax.shard_map(
        local,
        mesh=mesh,
        in_specs=placed,
        out_specs=(
            P(("dp", "upd"), None, None),
            P(("dp", "upd"), None, None),
            P(("dp", "upd"), None, None),
            P(None, ("dp", "upd"), None),
            P(None, ("dp", "upd"), None),
            P(None, ("dp", "upd"), None),
            P(None, ("dp", "upd"), None),
            P(None, ("dp", "upd")),
            P(None, ("dp", "upd")),
            P(),
            P(),
        ),
        check_vma=False,
    )
```

profile of v0, /device:TPU:0, one launch (start us, length us, event | category | flops | bytes accessed | tf_op | source)
XLA Modules:
  0.0 2761.8 jit_solution(14452595280854810627)
XLA Ops:
  28.9 67.6 %all-gather.8.cloned.1.call-done = bf16[8,768,768]{2,1,0:T(8,128)(2,1)} async-done(((bf16[8,24,768]{2,1,0:T(8,128)(2,1)}), bf16[8,768,768]{2,1,0:T(8,128)(2,1)}) %all-gather.8.cloned.1.call-update) | async-done | bytes 9437200 | tf_op jit(solution)/shard_map/all_gather | solution.py:184
  191.0 7.7 bitcast_reduce_fusion
  212.7 13.1 fusion.59
  225.8 35.1 %fusion.208 = (f32[8,128]{1,0:T(8,128)S(1)}, f32[8,128,3072]{2,1,0:T(8,128)S(1)}, f32[8,128,3072]{2,1,0:T(8,128)}) fusion(f32[8,128,3072]{2,1,0:T(8,128)} %get-tuple-element.100, f32[3072]{0:T(1024)S(1)} %bitcast.312, u8[128,3072]{1,0:T(8,128)(4,1)S(1)} %get-tuple-element.14, u8[128,3072]{1,0:T(8,128)(4,1)S(1)} %get-tuple-element.13), kind=kLoop, calls=%fused_computation.340 | loop fusion | flops 223345664 | bytes 38551552 | tf_op jit(solution)/shard_map/jvp()/reduce_sum | solution.py:57
  260.9 12.0 multiply_reduce_fusion.2
  273.0 8.2 multiply_reduce_fusion
  281.2 19.7 add_convert_fusion
  300.8 8.5 convolution_bitcast_fusion
  309.4 8.7 multiply_reduce_fusion.8
  326.9 6.9 pad_add_fusion
  344.7 6.5 convolution_convert_fusion.1
  351.3 12.2 multiply_reduce_fusion.1
  363.5 11.4 convert_reduce_fusion.1
  375.0 10.1 select_convert_fusion
  385.0 7.1 convolution_convert_fusion.6
  464.4 6.9 pad_add_fusion.1
  473.3 42.2 %psum.35 = f32[]{:T(128)} all-reduce(f32[]{:T(128)S(6)} %convert_element_type.296), channel_id=1, replica_groups=mesh['dp'=8,'upd'=4] {'dp','upd'}, use_global_device_ids=true, to_apply=%region_35.36 | all-reduce | flops 1 | bytes 8 | tf_op jit(solution)/shard_map/psum | solution.py:207
  549.2 200.3 %reduce-scatter.12.cloned.1.call-done = f32[8,24,768]{2,1,0:T(8,128)} async-done(((f32[8,768,768]{2,1,0:T(8,128)}), f32[8,24,768]{2,1,0:T(8,128)}) %reduce-scatter.12.cloned.1.call-update) | async-done | bytes 589840 | tf_op jit(solution)/shard_map/reduce_scatter | solution.py:211
  750.7 40.5 %all-reduce.31 = (f32[2]{0:T(128)S(1)}, f32[8]{0:T(128)S(1)}, f32[17,768]{1,0:T(8,128)}, f32[12]{0:T(128)}, f32[12,128]{1,0:T(8,128)}) all-reduce(f32[2]{0:T(128)S(1)} %get-tuple-element.61, f32[8]{0:T(128)S(1)} %get-tuple-element.59, f32[17,768]{1,0:T(8,128)S(1)} %pad_add_fusion.2, ...), channel_id=1, replica_groups=mesh['dp'=8,'upd'=4] {'dp','upd'}, use_global_device_ids=true, to_apply=%region_41.42 | all-reduce | flops 14614 | bytes 116912 | tf_op jit(solution)/shard_map/psum | solution.py:151
  791.2 15.9 fusion.177
  811.3 8.2 pad_maximum_fusion
  819.6 231.2 %reduce-scatter.16.cloned.1.call-done = f32[10,24,768]{2,1,0:T(8,128)} async-done(((f32[10,768,768]{2,1,0:T(8,128)}), f32[10,24,768]{2,1,0:T(8,128)}) %reduce-scatter.16.cloned.1.call-update) | async-done | bytes 737296 | tf_op jit(solution)/shard_map/reduce_scatter | solution.py:140
  1052.7 93.8 %all-gather.12.cloned.1.call-done = bf16[10,768,768]{2,1,0:T(8,128)(2,1)} async-done(((bf16[10,24,768]{2,1,0:T(8,128)(2,1)}), bf16[10,768,768]{2,1,0:T(8,128)(2,1)}) %all-gather.12.cloned.1.call-update) | async-done | bytes 11796496 | tf_op jit(solution)/shard_map/all_gather | solution.py:139
  1146.5 6.4 fusion.26
  1152.9 6.7 fusion.158
  1159.6 15.6 fusion.214
  1185.2 8.2 pad_maximum_fusion.1
  1193.5 229.9 %reduce-scatter.18.cloned.1.call-done = f32[10,24,768]{2,1,0:T(8,128)} async-done(((f32[10,768,768]{2,1,0:T(8,128)}), f32[10,24,768]{2,1,0:T(8,128)}) %reduce-scatter.18.cloned.1.call-update) | async-done | bytes 737296 | tf_op jit(solution)/shard_map/reduce_scatter | solution.py:140
  1425.3 93.5 %all-gather.14.cloned.1.call-done = bf16[10,768,768]{2,1,0:T(8,128)(2,1)} async-done(((bf16[10,24,768]{2,1,0:T(8,128)(2,1)}), bf16[10,768,768]{2,1,0:T(8,128)(2,1)}) %all-gather.14.cloned.1.call-update) | async-done | bytes 11796496 | tf_op jit(solution)/shard_map/all_gather | solution.py:139
  1518.8 6.3 fusion.22
  1525.1 6.7 fusion.155
  1531.8 15.6 fusion.216
  1557.2 8.2 pad_maximum_fusion.2
  1565.5 229.9 %reduce-scatter.20.cloned.1.call-done = f32[10,24,768]{2,1,0:T(8,128)} async-done(((f32[10,768,768]{2,1,0:T(8,128)}), f32[10,24,768]{2,1,0:T(8,128)}) %reduce-scatter.20.cloned.1.call-update) | async-done | bytes 737296 | tf_op jit(solution)/shard_map/reduce_scatter | solution.py:140
  1797.4 93.8 %all-gather.16.cloned.1.call-done = bf16[10,768,768]{2,1,0:T(8,128)(2,1)} async-done(((bf16[10,24,768]{2,1,0:T(8,128)(2,1)}), bf16[10,768,768]{2,1,0:T(8,128)(2,1)}) %all-gather.16.cloned.1.call-update) | async-done | bytes 11796496 | tf_op jit(solution)/shard_map/all_gather | solution.py:139
  1891.2 6.3 fusion.18
  1897.5 6.7 fusion.152
  1904.2 15.6 fusion.218
  1929.6 8.2 pad_maximum_fusion.3
  1937.9 229.9 %reduce-scatter.22.cloned.1.call-done = f32[10,24,768]{2,1,0:T(8,128)} async-done(((f32[10,768,768]{2,1,0:T(8,128)}), f32[10,24,768]{2,1,0:T(8,128)}) %reduce-scatter.22.cloned.1.call-update) | async-done | bytes 737296 | tf_op jit(solution)/shard_map/reduce_scatter | solution.py:140
  2169.8 93.4 %all-gather.18.cloned.1.call-done = bf16[10,768,768]{2,1,0:T(8,128)(2,1)} async-done(((bf16[10,24,768]{2,1,0:T(8,128)(2,1)}), bf16[10,768,768]{2,1,0:T(8,128)(2,1)}) %all-gather.18.cloned.1.call-update) | async-done | bytes 11796496 | tf_op jit(solution)/shard_map/all_gather | solution.py:139
  2269.4 6.7 fusion.149
  2276.2 15.6 fusion.220
  2301.6 8.2 pad_maximum_fusion.4
  2315.5 224.5 %reduce-scatter.24.cloned.1.call-done = f32[10,24,768]{2,1,0:T(8,128)} async-done(((f32[10,768,768]{2,1,0:T(8,128)}), f32[10,24,768]{2,1,0:T(8,128)}) %reduce-scatter.24.cloned.1.call-update) | async-done | bytes 737296 | tf_op jit(solution)/shard_map/reduce_scatter | solution.py:140
  2562.8 79.6 %reduce-scatter.26.cloned.1.call-done = f32[96,3]{1,0:T(8,128)} async-done(((f32[3072,3]{1,0:T(8,128)}), f32[96,3]{1,0:T(8,128)}) %reduce-scatter.26.cloned.1.call-update) | async-done | bytes 1168
  2646.3 90.7 %all-gather.20.cloned.1.call-done = bf16[10,768,768]{2,1,0:T(8,128)(2,1)} async-done(((bf16[10,24,768]{2,1,0:T(8,128)(2,1)}), bf16[10,768,768]{2,1,0:T(8,128)(2,1)}) %all-gather.20.cloned.1.call-update) | async-done | bytes 11796496 | tf_op jit(solution)/shard_map/all_gather | solution.py:139
  2740.3 7.5 fusion.10
  (496 shorter events, 356.7 us)
Async XLA Ops:
  7.2 147.8 %copy-start = (bf16[8,256,768]{2,1,0:T(8,128)(2,1)S(1)}, bf16[8,256,768]{2,1,0:T(8,128)(2,1)}, u32[]{:S(2)}) copy-start(bf16[8,256,768]{2,1,0:T(8,128)(2,1)} %param.14) | copy-start | bytes 9437188
  7.2 89.2 %all-gather.8.cloned.1.call-start = ((), (), s32[]{:S(2)}) async-start(), calls=%async_computation.8 | async-start | bytes 9732096 | tf_op jit(solution)/shard_map/all_gather | solution.py:184
  9.2 203.5 %all-gather.10.cloned.1.call-start = ((), (), s32[]{:S(2)}) async-start(), calls=%async_computation.9 | async-start | bytes 9732096 | tf_op jit(solution)/shard_map/all_gather | solution.py:185
  11.1 536.8 %reduce-scatter.14.cloned.1.call-start = ((), (), s32[]{:S(2)}) async-start(), calls=%async_computation.11 | async-start | bytes 19464192 | tf_op jit(solution)/shard_map/reduce_scatter | solution.py:212
  12.7 128.4 %copy-start.98 = (f32[768]{0:T(1024)}, f32[768]{0:T(1024)S(1)}, u32[]{:S(2)}) copy-start(f32[768]{0:T(1024)S(1)} %get-tuple-element.49) | copy-start | bytes 9220
  12.7 133.3 %copy-start.100 = (f32[768]{0:T(1024)}, f32[768]{0:T(1024)S(1)}, u32[]{:S(2)}) copy-start(f32[768]{0:T(1024)S(1)} %get-tuple-element.45) | copy-start | bytes 9220
  18.3 10.4 copy-start.102
  18.3 10.4 copy-start.122
  18.3 10.5 copy-start.103
  25.7 102.8 %copy-start.119 = (f32[12]{0:T(128)}, f32[12]{0:T(128)S(1)}, u32[]{:S(2)}) copy-start(f32[12]{0:T(128)S(1)} %convert_element_type.248) | copy-start | bytes 148
  28.7 87.0 %copy-start.74 = (pred[128,128]{0,1:T(8,128)(4,1)}, pred[128,128]{0,1:T(8,128)(4,1)S(1)}, u32[]{:S(2)}) copy-start(pred[128,128]{0,1:T(8,128)(4,1)S(1)} %iota_compare_fusion.7) | copy-start | bytes 49156
  225.8 35.1 %copy-start.45 = (bf16[8,128,768]{2,1,0:T(8,128)(2,1)S(1)}, bf16[8,128,768]{2,1,0:T(8,128)(2,1)}, u32[]{:S(2)}) copy-start(bf16[8,128,768]{2,1,0:T(8,128)(2,1)} %fusion.57) | copy-start | bytes 4718596
  300.8 20.7 slice-start.5
  309.4 12.2 slice-start.6
  333.8 415.6 %reduce-scatter.12.cloned.1.call-start = ((), (), s32[]{:S(2)}) async-start(), calls=%async_computation.10 | async-start | bytes 19464192 | tf_op jit(solution)/shard_map/reduce_scatter | solution.py:211
  351.2 12.3 slice-start
  351.2 12.2 slice-start.1
  351.2 12.2 slice-start.2
  446.7 14.9 copy-start.43
  471.4 46.5 %copy-start.32 = (bf16[8,12,64,256]{3,2,1,0:T(8,128)(2,1)S(1)}, bf16[8,12,64,256]{3,2,1,0:T(8,128)(2,1)}, u32[]{:S(2)}) copy-start(bf16[8,12,64,256]{3,2,1,0:T(8,128)(2,1)} %convolution_convert_fusion.1) | copy-start | bytes 9437188
  471.4 579.4 %reduce-scatter.16.cloned.1.call-start = ((), (), s32[]{:S(2)}) async-start(), calls=%async_computation.12 | async-start | bytes 24330240 | tf_op jit(solution)/shard_map/reduce_scatter | solution.py:140
  540.6 208.9 %copy-start.77 = (f32[8,24,768]{2,1,0:T(8,128)S(1)}, f32[8,24,768]{2,1,0:T(8,128)}, u32[]{:S(2)}) copy-start(f32[8,24,768]{2,1,0:T(8,128)} %param.20) | copy-start | bytes 1769476
  541.9 208.8 %copy-start.121 = (f32[12]{0:T(128)S(1)}, f32[12]{0:T(128)}, u32[]{:S(2)}) copy-start(f32[12]{0:T(128)} %get-tuple-element.82) | copy-start | bytes 148
  549.2 629.0 %copy-start.42 = (f32[2,96,768]{2,1,0:T(8,128)}, f32[2,96,768]{2,1,0:T(8,128)S(1)}, u32[]{:S(2)}) copy-start(f32[2,96,768]{2,1,0:T(8,128)S(1)} %get-tuple-element.62) | copy-start | bytes 1769476
  750.7 402.2 %copy-start.41 = (f32[8,24,768]{2,1,0:T(8,128)}, f32[8,24,768]{2,1,0:T(8,128)S(1)}, u32[]{:S(2)}) copy-start(f32[8,24,768]{2,1,0:T(8,128)S(1)} %get-tuple-element.60) | copy-start | bytes 1769476
  819.6 327.0 %all-gather.12.cloned.1.call-start = ((), (), s32[]{:S(2)}) async-start(), calls=%async_computation.13 | async-start | bytes 12165120 | tf_op jit(solution)/shard_map/all_gather | solution.py:139
  1052.7 370.6 %reduce-scatter.18.cloned.1.call-start = ((), (), s32[]{:S(2)}) async-start(), calls=%async_computation.14 | async-start | bytes 24330240 | tf_op jit(solution)/shard_map/reduce_scatter | solution.py:140
  1193.4 325.4 %all-gather.14.cloned.1.call-start = ((), (), s32[]{:S(2)}) async-start(), calls=%async_computation.15 | async-start | bytes 12165120 | tf_op jit(solution)/shard_map/all_gather | solution.py:139
  1425.2 370.2 %reduce-scatter.20.cloned.1.call-start = ((), (), s32[]{:S(2)}) async-start(), calls=%async_computation.16 | async-start | bytes 24330240 | tf_op jit(solution)/shard_map/reduce_scatter | solution.py:140
  1565.5 325.7 %all-gather.16.cloned.1.call-start = ((), (), s32[]{:S(2)}) async-start(), calls=%async_computation.17 | async-start | bytes 12165120 | tf_op jit(solution)/shard_map/all_gather | solution.py:139
  1797.4 370.5 %reduce-scatter.22.cloned.1.call-start = ((), (), s32[]{:S(2)}) async-start(), calls=%async_computation.18 | async-start | bytes 24330240 | tf_op jit(solution)/shard_map/reduce_scatter | solution.py:140
  1937.9 325.3 %all-gather.18.cloned.1.call-start = ((), (), s32[]{:S(2)}) async-start(), calls=%async_computation.19 | async-start | bytes 12165120 | tf_op jit(solution)/shard_map/all_gather | solution.py:139
  2169.7 370.2 %reduce-scatter.24.cloned.1.call-start = ((), (), s32[]{:S(2)}) async-start(), calls=%async_computation.20 | async-start | bytes 24330240 | tf_op jit(solution)/shard_map/reduce_scatter | solution.py:140
  2276.1 15.6 copy-start.28
  2297.6 12.3 copy-start.34
  2309.9 332.4 %reduce-scatter.26.cloned.1.call-start = ((), (), s32[]{:S(2)}) async-start(), calls=%async_computation.22 | async-start | bytes 1622016
  2313.6 228.2 %copy-start.113 = (f32[8,128]{1,0:T(8,128)S(1)}, f32[8,128]{1,0:T(8,128)}, u32[]{:S(2)}) copy-start(f32[8,128]{1,0:T(8,128)} %get-tuple-element.27) | copy-start | bytes 12292
  2313.7 228.2 %copy-start.7 = (bf16[8,128,768]{2,1,0:T(8,128)(2,1)S(1)}, bf16[8,128,768]{2,1,0:T(8,128)(2,1)}, u32[]{:S(2)}) copy-start(bf16[8,128,768]{2,1,0:T(8,128)(2,1)} %param.13) | copy-start | bytes 4718596
  2313.7 228.2 %copy-start.81 = (f32[8,128]{1,0:T(8,128)S(1)}, f32[8,128]{1,0:T(8,128)}, u32[]{:S(2)}) copy-start(f32[8,128]{1,0:T(8,128)} %copy-done.79) | copy-start | bytes 12292
  2313.7 228.2 %copy-start.88 = (f32[768]{0:T(1024)S(1)}, f32[768]{0:T(1024)}, u32[]{:S(2)}) copy-start(f32[768]{0:T(1024)} %copy-done.86) | copy-start | bytes 9220
  2313.7 228.2 %copy-start.91 = (f32[8,128]{1,0:T(8,128)S(1)}, f32[8,128]{1,0:T(8,128)}, u32[]{:S(2)}) copy-start(f32[8,128]{1,0:T(8,128)} %copy-done.89) | copy-start | bytes 12292
  2313.7 228.2 %copy-start.106 = (f32[8,128]{1,0:T(8,128)S(1)}, f32[8,128]{1,0:T(8,128)}, u32[]{:S(2)}) copy-start(f32[8,128]{1,0:T(8,128)} %copy-done.105) | copy-start | bytes 12292
  2315.5 421.6 %all-gather.20.cloned.1.call-start = ((), (), s32[]{:S(2)}) async-start(), calls=%async_computation.21 | async-start | bytes 12165120 | tf_op jit(solution)/shard_map/all_gather | solution.py:139
  2542.0 14.5 slice-start.7
  2556.5 88.7 %copy-start.127 = (f32[12]{0:T(128)S(1)}, f32[12]{0:T(128)}, u32[]{:S(2)}) copy-start(f32[12]{0:T(128)} %get-tuple-element.57) | copy-start | bytes 148
  2556.6 89.2 %copy-start.115 = (f32[12,128]{1,0:T(8,128)S(1)}, f32[12,128]{1,0:T(8,128)}, u32[]{:S(2)}) copy-start(f32[12,128]{1,0:T(8,128)} %get-tuple-element.58) | copy-start | bytes 18436
  2562.8 177.5 %copy-start.29 = (f32[8,24,768]{2,1,0:T(8,128)S(1)}, f32[8,24,768]{2,1,0:T(8,128)}, u32[]{:S(2)}) copy-start(f32[8,24,768]{2,1,0:T(8,128)} %copy-done.28) | copy-start | bytes 1769476
  2737.0 10.7 copy-start.17
  (107 other events, 436.5 us)
Sparse Core Ops, SparseCore 0:
  11.5 84.8 all-gather.7
  99.9 80.6 all-gather.9
  333.9 205.2 reduce-scatter.13
  545.5 203.8 reduce-scatter.11
  819.7 231.0 reduce-scatter.15
  1054.6 91.9 all-gather.11
  1193.5 229.7 reduce-scatter.17
  1426.8 91.9 all-gather.13
  1565.6 229.7 reduce-scatter.19
  1799.2 91.9 all-gather.15
  1938.0 229.7 reduce-scatter.21
  2171.2 91.9 all-gather.17
  2310.0 229.9 reduce-scatter.23
  2545.9 96.3 reduce-scatter.25
  2645.6 91.4 all-gather.19
where the time goes:
time: 2770 us; the launch traced here: 2760 us
  waiting for transfers between devices  1960 us (71%)
  matrix products  401 us (14%)
  other arithmetic  235 us (8%)
  blocking collectives  82.7 us (3%)
  local copies, waits for them, and re-layouts  65.6 us (2%)
    reduce_scatter x5, waiting for transfers between devices, both_grams(): lax.psum_scatter(joined, ('dp', 'upd'), scatter_dimension=1, tiled=True)  1150 us
    all_gather x5, waiting for transfers between devices, both_grams(): lax.all_gather(lax.psum_scatter(joined, ('dp', 'upd'), scatter_dimension=...  465 us
    reduce_scatter x1, waiting for transfers between devices, local(): lax.psum_scatter(square_slope, ('dp', 'upd'), scatter_dimension=1, tiled=...  200 us
    dot_general x10, matrix products, gram_of(): jnp.einsum('wrd,wre->wde', block, block, precision=lax.Precision.HIGHEST)  98.5 us
    unnamed x16, waiting for transfers between devices  79.8 us
    all_gather x1, waiting for transfers between devices, local(): lax.all_gather(square_master.astype(jnp.bfloat16), ('dp', 'upd'), axis=1,...  67.6 us
  transfers between devices with their start and end apart: 15, of which 13 were waited for; matrix products, arithmetic and copies ran while one was open for 12% of the time, Pallas kernels for 0%

commit v1 on v0

--- a/solution.py
+++ b/solution.py
@@ -15,6 +15,22 @@
 LEARN_RATE = 0.8
 WEIGHT_DECAY = 0.01
 NEGATIVE_LARGE = -1e30
+
+
+def define_the_wall(load, axis_tag, which_dim):
+    all_rows, opened, piece_next = (
+        lax.axis_size(axis_tag),
+        lax.axis_index(axis_tag),
+        load.shape[which_dim],
+    )
+    low, side_arr = (load, 1)
+    while side_arr < all_rows:
+        history = []
+        for dd in range(all_rows):
+            history.append((dd, (dd - side_arr) % all_rows))
+        low = jnp.concatenate([low, lax.ppermute(low, axis_tag, history)], which_dim)
+        side_arr = 2 * side_arr
+    return jnp.roll(low, opened * piece_next, which_dim)
 
 
 def plain_round(values):
@@ -136,13 +152,12 @@
 
 def both_grams(square, tall):
     joined = jnp.concatenate([gram_of(square), gram_of(tall)], axis=0)
-    summed = lax.all_gather(
+    summed = define_the_wall(
         lax.psum_scatter(joined, ("dp", "upd"), scatter_dimension=1, tiled=True).astype(
             jnp.bfloat16
         ),
         ("dp", "upd"),
-        axis=1,
-        tiled=True,
+        1,
     ).astype(jnp.float32)
     return (summed[:8], summed[8:])
 

time: 2770 us -> 4210 us (1.52)
  waiting for transfers between devices: 1960 us -> 3290 us
  local copies, waits for them, and re-layouts: 65.6 us -> 120 us
  other arithmetic: 235 us -> 285 us
    ppermute x0 -> x25, waiting for transfers between devices: none -> 1600 us  [define_the_wall(): lax.ppermute(low, axis_tag, history)]
    all_gather x5 -> x0, waiting for transfers between devices: 465 us -> none  [both_grams(): lax.all_gather(lax.psum_scatter(joined, ('dp', 'upd'), scatter_dimension=...]
    unnamed x16 -> x11, waiting for transfers between devices: 79.8 us -> 269 us
    concatenate x0 -> x20, other arithmetic: none -> 54 us  [the longest x5 52.1 us: define_the_wall(): return jnp.roll(low, opened * piece_next, which_dim)]
  transfers between devices with their start and end apart: 15 -> 35, of which waited for: 13 -> 32; matrix products, arithmetic and copies ran while one was open for 12% -> 8% of each run, Pallas kernels for 0% -> 0%
where the time goes in v1:
time: 4210 us; the launch traced here: 4200 us
  waiting for transfers between devices  3290 us (78%)
  matrix products  367 us (9%)
  other arithmetic  285 us (7%)
  local copies, waits for them, and re-layouts  120 us (3%)
  blocking collectives  82.7 us (2%)
    ppermute x25, waiting for transfers between devices, define_the_wall(): lax.ppermute(low, axis_tag, history)  1600 us
    reduce_scatter x5, waiting for transfers between devices, both_grams(): lax.psum_scatter(joined, ('dp', 'upd'), scatter_dimension=1, tiled=True)  1160 us
    unnamed x11, waiting for transfers between devices  269 us
    reduce_scatter x1, waiting for transfers between devices, local(): lax.psum_scatter(square_slope, ('dp', 'upd'), scatter_dimension=1, tiled=...  200 us
    dot_general x10, matrix products, gram_of(): jnp.einsum('wrd,wre->wde', block, block, precision=lax.Precision.HIGHEST)  99.4 us
  transfers between devices with their start and end apart: 35, of which 32 were waited for; matrix products, arithmetic and copies ran while one was open for 8% of the time, Pallas kernels for 0%

profile of v1, /device:TPU:0, one launch (start us, length us, event | category | flops | bytes accessed | tf_op | source)
XLA Modules:
  0.0 4196.4 jit_solution(2254900155985637613)
XLA Ops:
  28.9 67.6 %all-gather.3.cloned.1.call-done = bf16[8,768,768]{2,1,0:T(8,128)(2,1)} async-done(((bf16[8,24,768]{2,1,0:T(8,128)(2,1)}), bf16[8,768,768]{2,1,0:T(8,128)(2,1)}) %all-gather.3.cloned.1.call-update) | async-done | bytes 9437200 | tf_op jit(solution)/shard_map/all_gather | solution.py:199
  212.7 13.1 fusion.64
  225.8 35.1 fusion.191
  260.9 12.0 multiply_reduce_fusion.2
  281.2 19.7 add_convert_fusion
  300.9 8.5 convolution_bitcast_fusion
  309.4 8.7 multiply_reduce_fusion.8
  351.3 12.2 multiply_reduce_fusion.1
  363.5 11.4 convert_reduce_fusion.1
  375.0 10.1 select_convert_fusion
  473.3 42.1 %psum.35 = f32[]{:T(128)} all-reduce(f32[]{:T(128)S(6)} %convert_element_type.296), channel_id=1, replica_groups=mesh['dp'=8,'upd'=4] {'dp','upd'}, use_global_device_ids=true, to_apply=%region_35.36 | all-reduce | flops 1 | bytes 8 | tf_op jit(solution)/shard_map/psum | solution.py:222
  549.2 200.4 %reduce-scatter.12.cloned.1.call-done = f32[8,24,768]{2,1,0:T(8,128)} async-done(((f32[8,768,768]{2,1,0:T(8,128)}), f32[8,24,768]{2,1,0:T(8,128)}) %reduce-scatter.12.cloned.1.call-update) | async-done | bytes 589840 | tf_op jit(solution)/shard_map/reduce_scatter | solution.py:226
  750.9 40.5 all-reduce.31
  791.4 15.9 fusion.140
  819.8 231.1 %reduce-scatter.16.cloned.1.call-done = f32[10,24,768]{2,1,0:T(8,128)} async-done(((f32[10,768,768]{2,1,0:T(8,128)}), f32[10,24,768]{2,1,0:T(8,128)}) %reduce-scatter.16.cloned.1.call-update) | async-done | bytes 737296 | tf_op jit(solution)/shard_map/reduce_scatter | solution.py:156
  1061.9 16.5 collective-permute-done.1
  1078.6 34.7 collective-permute-done.2
  1119.8 59.2 %collective-permute-done.3 = bf16[10,192,768]{2,1,0:T(8,128)(2,1)S(1)} collective-permute-done((bf16[10,192,768]{2,1,0:T(8,128)(2,1)S(1)}, bf16[10,192,768]{2,1,0:T(8,128)(2,1)S(1)}, u32[]{:S(2)}, u32[]{:S(2)}) %collective-permute-start.3) | collective-permute-done | bytes 2949152 | tf_op jit(solution)/shard_map/ppermute | solution.py:31
  1183.1 254.6 %collective-permute-done.4 = bf16[10,384,768]{2,1,0:T(8,128)(2,1)} collective-permute-done((bf16[10,384,768]{2,1,0:T(8,128)(2,1)}, bf16[10,384,768]{2,1,0:T(8,128)(2,1)}, u32[]{:S(2)}, u32[]{:S(2)}) %collective-permute-start.4) | collective-permute-done | bytes 5898272 | tf_op jit(solution)/shard_map/ppermute | solution.py:31
  1443.3 10.4 fusion.10
  1462.8 15.8 fusion.197
  1492.4 231.8 %reduce-scatter.18.cloned.1.call-done = f32[10,24,768]{2,1,0:T(8,128)} async-done(((f32[10,768,768]{2,1,0:T(8,128)}), f32[10,24,768]{2,1,0:T(8,128)}) %reduce-scatter.18.cloned.1.call-update) | async-done | bytes 737296 | tf_op jit(solution)/shard_map/reduce_scatter | solution.py:156
  1734.4 16.4 collective-permute-done.6
  1751.0 34.8 collective-permute-done.7
  1791.4 60.3 %collective-permute-done.8 = bf16[10,192,768]{2,1,0:T(8,128)(2,1)S(1)} collective-permute-done((bf16[10,192,768]{2,1,0:T(8,128)(2,1)S(1)}, bf16[10,192,768]{2,1,0:T(8,128)(2,1)S(1)}, u32[]{:S(2)}, u32[]{:S(2)}) %collective-permute-start.8) | collective-permute-done | bytes 2949152 | tf_op jit(solution)/shard_map/ppermute | solution.py:31
  1854.4 254.4 %collective-permute-done.9 = bf16[10,384,768]{2,1,0:T(8,128)(2,1)S(1)} collective-permute-done((bf16[10,384,768]{2,1,0:T(8,128)(2,1)S(1)}, bf16[10,384,768]{2,1,0:T(8,128)(2,1)S(1)}, u32[]{:S(2)}, u32[]{:S(2)}) %collective-permute-start.9) | collective-permute-done | bytes 5898272 | tf_op jit(solution)/shard_map/ppermute | solution.py:31
  2111.8 10.4 fusion.9
  2131.2 15.8 fusion.199
  2160.8 231.7 %reduce-scatter.20.cloned.1.call-done = f32[10,24,768]{2,1,0:T(8,128)} async-done(((f32[10,768,768]{2,1,0:T(8,128)}), f32[10,24,768]{2,1,0:T(8,128)}) %reduce-scatter.20.cloned.1.call-update) | async-done | bytes 737296 | tf_op jit(solution)/shard_map/reduce_scatter | solution.py:156
  2402.8 16.5 collective-permute-done.11
  2419.5 34.7 collective-permute-done.12
  2459.7 60.2 %collective-permute-done.13 = bf16[10,192,768]{2,1,0:T(8,128)(2,1)S(1)} collective-permute-done((bf16[10,192,768]{2,1,0:T(8,128)(2,1)S(1)}, bf16[10,192,768]{2,1,0:T(8,128)(2,1)S(1)}, u32[]{:S(2)}, u32[]{:S(2)}) %collective-permute-start.13) | collective-permute-done | bytes 2949152 | tf_op jit(solution)/shard_map/ppermute | solution.py:31
  2522.7 254.4 %collective-permute-done.14 = bf16[10,384,768]{2,1,0:T(8,128)(2,1)S(1)} collective-permute-done((bf16[10,384,768]{2,1,0:T(8,128)(2,1)S(1)}, bf16[10,384,768]{2,1,0:T(8,128)(2,1)S(1)}, u32[]{:S(2)}, u32[]{:S(2)}) %collective-permute-start.14) | collective-permute-done | bytes 5898272 | tf_op jit(solution)/shard_map/ppermute | solution.py:31
  2780.0 10.4 fusion.8
  2799.5 15.8 fusion.201
  2829.1 231.9 %reduce-scatter.22.cloned.1.call-done = f32[10,24,768]{2,1,0:T(8,128)} async-done(((f32[10,768,768]{2,1,0:T(8,128)}), f32[10,24,768]{2,1,0:T(8,128)}) %reduce-scatter.22.cloned.1.call-update) | async-done | bytes 737296 | tf_op jit(solution)/shard_map/reduce_scatter | solution.py:156
  3071.2 16.4 collective-permute-done.16
  3087.7 34.8 collective-permute-done.17
  3128.1 60.3 %collective-permute-done.18 = bf16[10,192,768]{2,1,0:T(8,128)(2,1)S(1)} collective-permute-done((bf16[10,192,768]{2,1,0:T(8,128)(2,1)S(1)}, bf16[10,192,768]{2,1,0:T(8,128)(2,1)S(1)}, u32[]{:S(2)}, u32[]{:S(2)}) %collective-permute-start.18) | collective-permute-done | bytes 2949152 | tf_op jit(solution)/shard_map/ppermute | solution.py:31
  3191.1 254.4 %collective-permute-done.19 = bf16[10,384,768]{2,1,0:T(8,128)(2,1)S(1)} collective-permute-done((bf16[10,384,768]{2,1,0:T(8,128)(2,1)S(1)}, bf16[10,384,768]{2,1,0:T(8,128)(2,1)S(1)}, u32[]{:S(2)}, u32[]{:S(2)}) %collective-permute-start.19) | collective-permute-done | bytes 5898272 | tf_op jit(solution)/shard_map/ppermute | solution.py:31
  3448.4 10.4 fusion.7
  3467.9 15.9 fusion.203
  3497.5 232.0 %reduce-scatter.24.cloned.1.call-done = f32[10,24,768]{2,1,0:T(8,128)} async-done(((f32[10,768,768]{2,1,0:T(8,128)}), f32[10,24,768]{2,1,0:T(8,128)}) %reduce-scatter.24.cloned.1.call-update) | async-done | bytes 737296 | tf_op jit(solution)/shard_map/reduce_scatter | solution.py:156
  3740.4 16.4 collective-permute-done.21
  3756.9 34.8 collective-permute-done.22
  3798.3 59.2 %collective-permute-done.23 = bf16[10,192,768]{2,1,0:T(8,128)(2,1)S(1)} collective-permute-done((bf16[10,192,768]{2,1,0:T(8,128)(2,1)S(1)}, bf16[10,192,768]{2,1,0:T(8,128)(2,1)S(1)}, u32[]{:S(2)}, u32[]{:S(2)}) %collective-permute-start.23) | collective-permute-done | bytes 2949152 | tf_op jit(solution)/shard_map/ppermute | solution.py:31
  3888.5 268.4 %reduce-scatter.26.cloned.1.call-done = f32[96,3]{1,0:T(8,128)} async-done(((f32[3072,3]{1,0:T(8,128)}), f32[96,3]{1,0:T(8,128)}) %reduce-scatter.26.cloned.1.call-update) | async-done | bytes 1168
  4166.5 10.4 fusion.6
  (574 shorter events, 565.6 us)
Async XLA Ops:
  7.2 147.8 %copy-start = (bf16[8,256,768]{2,1,0:T(8,128)(2,1)S(1)}, bf16[8,256,768]{2,1,0:T(8,128)(2,1)}, u32[]{:S(2)}) copy-start(bf16[8,256,768]{2,1,0:T(8,128)(2,1)} %param.16) | copy-start | bytes 9437188
  7.2 89.2 %all-gather.3.cloned.1.call-start = ((), (), s32[]{:S(2)}) async-start(), calls=%async_computation.8 | async-start | bytes 9732096 | tf_op jit(solution)/shard_map/all_gather | solution.py:199
  9.2 203.5 %all-gather.5.cloned.1.call-start = ((), (), s32[]{:S(2)}) async-start(), calls=%async_computation.9 | async-start | bytes 9732096 | tf_op jit(solution)/shard_map/all_gather | solution.py:200
  11.1 536.8 %reduce-scatter.14.cloned.1.call-start = ((), (), s32[]{:S(2)}) async-start(), calls=%async_computation.11 | async-start | bytes 19464192 | tf_op jit(solution)/shard_map/reduce_scatter | solution.py:227
  12.7 128.4 %copy-start.97 = (f32[768]{0:T(1024)}, f32[768]{0:T(1024)S(1)}, u32[]{:S(2)}) copy-start(f32[768]{0:T(1024)S(1)} %get-tuple-element.50) | copy-start | bytes 9220
  12.7 133.3 %copy-start.99 = (f32[768]{0:T(1024)}, f32[768]{0:T(1024)S(1)}, u32[]{:S(2)}) copy-start(f32[768]{0:T(1024)S(1)} %get-tuple-element.46) | copy-start | bytes 9220
  25.7 102.8 %copy-start.118 = (f32[12]{0:T(128)}, f32[12]{0:T(128)S(1)}, u32[]{:S(2)}) copy-start(f32[12]{0:T(128)S(1)} %convert_element_type.248) | copy-start | bytes 148
  28.7 87.0 %copy-start.73 = (pred[128,128]{0,1:T(8,128)(4,1)}, pred[128,128]{0,1:T(8,128)(4,1)S(1)}, u32[]{:S(2)}) copy-start(pred[128,128]{0,1:T(8,128)(4,1)S(1)} %iota_compare_fusion.7) | copy-start | bytes 49156
  333.8 415.8 %reduce-scatter.12.cloned.1.call-start = ((), (), s32[]{:S(2)}) async-start(), calls=%async_computation.10 | async-start | bytes 19464192 | tf_op jit(solution)/shard_map/reduce_scatter | solution.py:226
  471.4 579.5 %reduce-scatter.16.cloned.1.call-start = ((), (), s32[]{:S(2)}) async-start(), calls=%async_computation.12 | async-start | bytes 24330240 | tf_op jit(solution)/shard_map/reduce_scatter | solution.py:156
  540.6 209.1 %copy-start.76 = (f32[8,24,768]{2,1,0:T(8,128)S(1)}, f32[8,24,768]{2,1,0:T(8,128)}, u32[]{:S(2)}) copy-start(f32[8,24,768]{2,1,0:T(8,128)} %param.22) | copy-start | bytes 1769476
  541.9 209.0 %copy-start.120 = (f32[12]{0:T(128)S(1)}, f32[12]{0:T(128)}, u32[]{:S(2)}) copy-start(f32[12]{0:T(128)} %get-tuple-element.93) | copy-start | bytes 148
  549.2 929.4 %copy-start.41 = (f32[2,96,768]{2,1,0:T(8,128)}, f32[2,96,768]{2,1,0:T(8,128)S(1)}, u32[]{:S(2)}) copy-start(f32[2,96,768]{2,1,0:T(8,128)S(1)} %get-tuple-element.73) | copy-start | bytes 1769476
  750.9 708.0 %copy-start.40 = (f32[8,24,768]{2,1,0:T(8,128)}, f32[8,24,768]{2,1,0:T(8,128)S(1)}, u32[]{:S(2)}) copy-start(f32[8,24,768]{2,1,0:T(8,128)S(1)} %get-tuple-element.71) | copy-start | bytes 1769476
  819.8 904.4 %reduce-scatter.18.cloned.1.call-start = ((), (), s32[]{:S(2)}) async-start(), calls=%async_computation.13 | async-start | bytes 24330240 | tf_op jit(solution)/shard_map/reduce_scatter | solution.py:156
  1052.8 8.4 collective-permute-start
  1061.3 17.1 collective-permute-start.1
  1078.5 34.7 collective-permute-start.2
  1113.5 65.5 %collective-permute-start.3 = (bf16[10,192,768]{2,1,0:T(8,128)(2,1)S(1)}, bf16[10,192,768]{2,1,0:T(8,128)(2,1)S(1)}, u32[]{:S(2)}, u32[]{:S(2)}) collective-permute-start(bf16[10,192,768]{2,1,0:T(8,128)(2,1)S(1)} %pad_maximum_fusion.5), channel_id=1, source_target_pairs={{0,24},{1,25},{2,26},{3,27},{4,28},{5,29},{6,30},{7,31},{8,0},{9,1... | collective-permute-start | bytes 8847368 | tf_op jit(solution)/shard_map/ppermute | solution.py:31
  1182.3 255.4 %collective-permute-start.4 = (bf16[10,384,768]{2,1,0:T(8,128)(2,1)}, bf16[10,384,768]{2,1,0:T(8,128)(2,1)}, u32[]{:S(2)}, u32[]{:S(2)}) collective-permute-start(bf16[10,384,768]{2,1,0:T(8,128)(2,1)} %get-tuple-element.103), channel_id=1, source_target_pairs={{0,16},{1,17},{2,18},{3,19},{4,20},{5,21},{6,22},{7,23},{8,24},{9,... | collective-permute-start | bytes 17694728 | tf_op jit(solution)/shard_map/ppermute | solution.py:31
  1492.4 900.1 %reduce-scatter.20.cloned.1.call-start = ((), (), s32[]{:S(2)}) async-start(), calls=%async_computation.14 | async-start | bytes 24330240 | tf_op jit(solution)/shard_map/reduce_scatter | solution.py:156
  1725.3 8.4 collective-permute-start.5
  1733.8 17.0 collective-permute-start.6
  1750.9 34.9 collective-permute-start.7
  1786.0 65.7 %collective-permute-start.8 = (bf16[10,192,768]{2,1,0:T(8,128)(2,1)S(1)}, bf16[10,192,768]{2,1,0:T(8,128)(2,1)S(1)}, u32[]{:S(2)}, u32[]{:S(2)}) collective-permute-start(bf16[10,192,768]{2,1,0:T(8,128)(2,1)S(1)} %pad_maximum_fusion.6), channel_id=1, source_target_pairs={{0,24},{1,25},{2,26},{3,27},{4,28},{5,29},{6,30},{7,31},{8,0},{9,1... | collective-permute-start | bytes 8847368 | tf_op jit(solution)/shard_map/ppermute | solution.py:31
  1853.7 255.0 %collective-permute-start.9 = (bf16[10,384,768]{2,1,0:T(8,128)(2,1)S(1)}, bf16[10,384,768]{2,1,0:T(8,128)(2,1)S(1)}, u32[]{:S(2)}, u32[]{:S(2)}) collective-permute-start(bf16[10,384,768]{2,1,0:T(8,128)(2,1)S(1)} %get-tuple-element.101), channel_id=1, source_target_pairs={{0,16},{1,17},{2,18},{3,19},{4,20},{5,21},{6,22},{7,23},{8,24},{9,... | collective-permute-start | bytes 17694728 | tf_op jit(solution)/shard_map/ppermute | solution.py:31
  2160.7 900.3 %reduce-scatter.22.cloned.1.call-start = ((), (), s32[]{:S(2)}) async-start(), calls=%async_computation.15 | async-start | bytes 24330240 | tf_op jit(solution)/shard_map/reduce_scatter | solution.py:156
  2393.7 8.5 collective-permute-start.10
  2402.2 17.1 collective-permute-start.11
  2419.4 34.7 collective-permute-start.12
  2454.4 65.6 %collective-permute-start.13 = (bf16[10,192,768]{2,1,0:T(8,128)(2,1)S(1)}, bf16[10,192,768]{2,1,0:T(8,128)(2,1)S(1)}, u32[]{:S(2)}, u32[]{:S(2)}) collective-permute-start(bf16[10,192,768]{2,1,0:T(8,128)(2,1)S(1)} %pad_maximum_fusion.7), channel_id=1, source_target_pairs={{0,24},{1,25},{2,26},{3,27},{4,28},{5,29},{6,30},{7,31},{8,0},{9,1... | collective-permute-start | bytes 8847368 | tf_op jit(solution)/shard_map/ppermute | solution.py:31
  2522.0 255.1 %collective-permute-start.14 = (bf16[10,384,768]{2,1,0:T(8,128)(2,1)S(1)}, bf16[10,384,768]{2,1,0:T(8,128)(2,1)S(1)}, u32[]{:S(2)}, u32[]{:S(2)}) collective-permute-start(bf16[10,384,768]{2,1,0:T(8,128)(2,1)S(1)} %get-tuple-element.99), channel_id=1, source_target_pairs={{0,16},{1,17},{2,18},{3,19},{4,20},{5,21},{6,22},{7,23},{8,24},{9,... | collective-permute-start | bytes 17694728 | tf_op jit(solution)/shard_map/ppermute | solution.py:31
  2829.0 900.5 %reduce-scatter.24.cloned.1.call-start = ((), (), s32[]{:S(2)}) async-start(), calls=%async_computation.16 | async-start | bytes 24330240 | tf_op jit(solution)/shard_map/reduce_scatter | solution.py:156
  3062.2 8.3 collective-permute-start.15
  3070.5 17.0 collective-permute-start.16
  3087.7 34.9 collective-permute-start.17
  3122.8 65.7 %collective-permute-start.18 = (bf16[10,192,768]{2,1,0:T(8,128)(2,1)S(1)}, bf16[10,192,768]{2,1,0:T(8,128)(2,1)S(1)}, u32[]{:S(2)}, u32[]{:S(2)}) collective-permute-start(bf16[10,192,768]{2,1,0:T(8,128)(2,1)S(1)} %pad_maximum_fusion.8), channel_id=1, source_target_pairs={{0,24},{1,25},{2,26},{3,27},{4,28},{5,29},{6,30},{7,31},{8,0},{9,1... | collective-permute-start | bytes 8847368 | tf_op jit(solution)/shard_map/ppermute | solution.py:31
  3190.5 255.0 %collective-permute-start.19 = (bf16[10,384,768]{2,1,0:T(8,128)(2,1)S(1)}, bf16[10,384,768]{2,1,0:T(8,128)(2,1)S(1)}, u32[]{:S(2)}, u32[]{:S(2)}) collective-permute-start(bf16[10,384,768]{2,1,0:T(8,128)(2,1)S(1)} %get-tuple-element.97), channel_id=1, source_target_pairs={{0,16},{1,17},{2,18},{3,19},{4,20},{5,21},{6,22},{7,23},{8,24},{9,... | collective-permute-start | bytes 17694728 | tf_op jit(solution)/shard_map/ppermute | solution.py:31
  3467.8 710.4 %copy-start.28 = (f32[8,24,768]{2,1,0:T(8,128)}, f32[8,24,768]{2,1,0:T(8,128)S(1)}, u32[]{:S(2)}) copy-start(f32[8,24,768]{2,1,0:T(8,128)S(1)} %add_add_fusion.11) | copy-start | bytes 1769476
  3485.2 691.7 %copy-start.32 = (f32[2,96,768]{2,1,0:T(8,128)}, f32[2,96,768]{2,1,0:T(8,128)S(1)}, u32[]{:S(2)}) copy-start(f32[2,96,768]{2,1,0:T(8,128)S(1)} %add_add_fusion.10) | copy-start | bytes 1769476
  3497.5 659.4 %reduce-scatter.26.cloned.1.call-start = ((), (), s32[]{:S(2)}) async-start(), calls=%async_computation.17 | async-start | bytes 1622016
  3731.4 8.3 collective-permute-start.20
  3739.7 17.0 collective-permute-start.21
  3756.8 34.9 collective-permute-start.22
  3792.0 65.6 %collective-permute-start.23 = (bf16[10,192,768]{2,1,0:T(8,128)(2,1)S(1)}, bf16[10,192,768]{2,1,0:T(8,128)(2,1)S(1)}, u32[]{:S(2)}, u32[]{:S(2)}) collective-permute-start(bf16[10,192,768]{2,1,0:T(8,128)(2,1)S(1)} %pad_maximum_fusion.9), channel_id=1, source_target_pairs={{0,24},{1,25},{2,26},{3,27},{4,28},{5,29},{6,30},{7,31},{8,0},{9,1... | collective-permute-start | bytes 8847368 | tf_op jit(solution)/shard_map/ppermute | solution.py:31
  3860.8 300.1 %collective-permute-start.24 = (bf16[10,384,768]{2,1,0:T(8,128)(2,1)}, bf16[10,384,768]{2,1,0:T(8,128)(2,1)}, u32[]{:S(2)}, u32[]{:S(2)}) collective-permute-start(bf16[10,384,768]{2,1,0:T(8,128)(2,1)} %get-tuple-element.95), channel_id=1, source_target_pairs={{0,16},{1,17},{2,18},{3,19},{4,20},{5,21},{6,22},{7,23},{8,24},{9,... | collective-permute-start | bytes 17694728 | tf_op jit(solution)/shard_map/ppermute | solution.py:31
  3886.3 273.5 %copy-start.126 = (f32[12]{0:T(128)S(1)}, f32[12]{0:T(128)}, u32[]{:S(2)}) copy-start(f32[12]{0:T(128)} %get-tuple-element.58) | copy-start | bytes 148
  3886.3 274.0 %copy-start.114 = (f32[12,128]{1,0:T(8,128)S(1)}, f32[12,128]{1,0:T(8,128)}, u32[]{:S(2)}) copy-start(f32[12,128]{1,0:T(8,128)} %get-tuple-element.59) | copy-start | bytes 18436
  (124 other events, 675.3 us)
Sparse Core Ops, SparseCore 0:
  11.5 84.8 all-gather.2
  99.9 80.6 all-gather.4
  334.0 205.2 reduce-scatter.13
  545.5 204.0 reduce-scatter.11
  819.9 230.9 reduce-scatter.15
  1492.5 231.6 reduce-scatter.17
  2160.9 231.5 reduce-scatter.19
  2829.1 231.8 reduce-scatter.21
  3497.6 231.8 reduce-scatter.23
  3867.1 289.7 reduce-scatter.25
